TPU v7x, 32 devices: a whole 2x2x4 slice. The times are simulated.
32 devices in a mesh: shard: 2 (over x), ctx: 4 (over y, core), tp: 4 (over z).
Axes of the slice: x: 2, y: 2, z: 4, core: 2. Of those that a mesh axis runs over, the one named last changes fastest.
Arguments:
- tokens: bfloat16 [4, 4096, 1024], P('shard', ('ctx', 'tp')), may hold values from -6 to 6
- positions: int32 [4, 4096], P('shard', 'ctx'), may hold values from 0 to 12287, as said below
- first_gain: float32 [1024], replicated, may hold values from 0.5 to 1.5
- query_weight: bfloat16 [1024, 1024], P(('shard', 'ctx'), 'tp'), may hold values from -0.1875 to 0.1875
- key_weight: bfloat16 [1024, 512], P(('shard', 'ctx'), 'tp'), may hold values from -0.1875 to 0.1875
- value_weight: bfloat16 [1024, 512], P(('shard', 'ctx'), 'tp'), may hold values from -0.1875 to 0.1875
- query_gain: float32 [64], replicated, may hold values from 0.1 to 1.9
- key_gain: float32 [64], replicated, may hold values from 0.1 to 1.9
- output_weight: bfloat16 [1024, 1024], P('tp', ('shard', 'ctx')), may hold values from -1 to 1
- second_gain: float32 [1024], replicated, may hold values from 0.5 to 1.5
- gate_weight: bfloat16 [1024, 4608], P(('shard', 'ctx'), 'tp'), may hold values from -0.1875 to 0.1875
- up_weight: bfloat16 [1024, 4608], P(('shard', 'ctx'), 'tp'), may hold values from -0.1875 to 0.1875
- down_weight: bfloat16 [4608, 1024], P('tp', ('shard', 'ctx')), may hold values from -0.09375 to 0.09375
- upstream: bfloat16 [4, 4096, 1024], P('shard', ('ctx', 'tp')), may hold values from -6 to 6
Outputs:
- block_output: bfloat16 [4, 4096, 1024], P('shard', ('ctx', 'tp'))
- token_gradient: float32 [4, 4096, 1024], P('shard', ('ctx', 'tp'))
- query_gradient: float32 [1024, 1024], P(('shard', 'ctx'), 'tp')
- key_gradient: float32 [1024, 512], P(('shard', 'ctx'), 'tp')
- value_gradient: float32 [1024, 512], P(('shard', 'ctx'), 'tp')
- output_gradient: float32 [1024, 1024], P('tp', ('shard', 'ctx'))
- gate_gradient: float32 [1024, 4608], P(('shard', 'ctx'), 'tp')
- up_gradient: float32 [1024, 4608], P(('shard', 'ctx'), 'tp')
- down_gradient: float32 [4608, 1024], P('tp', ('shard', 'ctx'))
- first_gain_gradient: float32 [1024], replicated
- second_gain_gradient: float32 [1024], replicated
- query_gain_gradient: float32 [64], replicated
- key_gain_gradient: float32 [64], replicated
Inputs may be any that keep to these rules, and one draw needn't show every extreme that they name: `positions`: along each sequence a position exceeds the one before it by 1 to 3; the first is at most 2.
All inputs are finite; a program needn't handle non-finite values.
Results may differ from a plain program's by a relative error of at most 0.02.
Values may be sent and summed in bfloat16 or wider, within the bound.
No kernel may reach another device: no remote copies, remote signals or barrier semaphores. Data moves between devices by JAX's collectives and lax.ppermute only.
A program may use at most 192 MiB of HBM per device.

v0:
```python
import math
import jax
import jax.numpy as jnp
from jax import lax
from jax.sharding import PartitionSpec as P

EPS = 1e-05
THETA = 1000000.0
NEGATIVE = -1e30


def norm_rows(values, gain):
    return values * lax.rsqrt(jnp.mean(values * values, axis=-1, keepdims=True) + EPS) * gain


def rotary_tables(places, width):
    freqs = jnp.exp(-math.log(THETA) * jnp.arange(0, width, 2).astype(jnp.float32) / width)
    angles = places.astype(jnp.float32)[:, None] * freqs[None, :]
    cosine = jnp.concatenate([jnp.cos(angles), jnp.cos(angles)], axis=-1)[:, None, :]
    sine = jnp.concatenate([jnp.sin(angles), jnp.sin(angles)], axis=-1)[:, None, :]
    return (cosine, sine)


def shape_heads(raw, gain, cosine, sine):
    normed = norm_rows(raw, gain)
    half = normed.shape[-1] // 2
    turned = jnp.concatenate([-normed[..., half:], normed[..., :half]], axis=-1)
    return normed * cosine + turned * sine


def dot_first(left, right):
    return lax.dot_general(
        left, right, (((0,), (0,)), ((), ())), preferred_element_type=jnp.float32
    )


def dot_last(left, right):
    return lax.dot_general(
        left, right, (((1,), (1,)), ((), ())), preferred_element_type=jnp.float32
    )


def project_rows(left, right):
    return jnp.dot(left, right, preferred_element_type=jnp.float32)


def project_pair(gate_back, gate_full, up_back, up_full):
    first_part = dot_last(gate_back, gate_full)
    return first_part + dot_last(up_back, up_full)


def project_three(query_back, query_full, key_back, key_full, value_back, value_full):
    total = dot_last(query_back, query_full)
    total = total + dot_last(key_back, key_full)
    return total + dot_last(value_back, value_full)


def fetch_weights(
    query_weight, key_weight, value_weight, output_weight, gate_weight, up_weight, down_weight
):
    return (
        lax.all_gather(query_weight, ("shard", "ctx"), axis=0, tiled=True),
        lax.all_gather(key_weight, ("shard", "ctx"), axis=0, tiled=True),
        lax.all_gather(value_weight, ("shard", "ctx"), axis=0, tiled=True),
        lax.all_gather(output_weight, ("shard", "ctx"), axis=1, tiled=True),
        lax.all_gather(gate_weight, ("shard", "ctx"), axis=0, tiled=True),
        lax.all_gather(up_weight, ("shard", "ctx"), axis=0, tiled=True),
        lax.all_gather(down_weight, ("shard", "ctx"), axis=1, tiled=True),
    )


def attend(query_b, key_b, value_b, first_query):
    span_rows, kv_heads, group, width = query_b.shape
    scale = 1.0 / math.sqrt(width)
    query_index = first_query + jnp.arange(span_rows)
    last_query = first_query + span_rows - 1
    init = (
        jnp.full((kv_heads, group, span_rows), NEGATIVE, jnp.float32),
        jnp.zeros((kv_heads, group, span_rows), jnp.float32),
        jnp.zeros((kv_heads, group, span_rows, width), jnp.float32),
    )
    key_piece = lax.all_gather(key_b, "ctx", axis=0, tiled=True)
    value_piece = lax.all_gather(value_b, "ctx", axis=0, tiled=True)

    def update(state):
        peak, total, accum = state
        scores = (
            jnp.einsum("qkgd,nkd->kgqn", query_b, key_piece, preferred_element_type=jnp.float32)
            * scale
        )
        key_index = jnp.arange(key_piece.shape[0])
        allowed = key_index[None, :] <= query_index[:, None]
        masked = jnp.where(allowed, scores, NEGATIVE)
        new_peak = jnp.maximum(peak, jnp.max(masked, axis=-1))
        weights = jnp.where(allowed, jnp.exp(masked - new_peak[..., None]), 0.0)
        total = jnp.sum(weights, axis=-1)
        accum = jnp.einsum(
            "kgqn,nkd->kgqd",
            weights.astype(jnp.bfloat16),
            value_piece,
            preferred_element_type=jnp.float32,
        )
        return (new_peak, total, accum)

    peak, total, accum = lax.cond(jnp.int32(0) <= last_query, update, lambda state: state, init)
    return (accum / total[..., None], peak + jnp.log(total))


def attend_back(query_b, keys_all, values_all, back_b, attention, logsum, first_query):
    span_rows, kv_heads, group, width = query_b.shape
    scale = 1.0 / math.sqrt(width)
    query_index = first_query + jnp.arange(span_rows)
    delta = jnp.einsum("qkgd,kgqd->kgq", back_b.astype(jnp.float32), attention)

    def block(index, carry):
        query_back, key_buffer, value_buffer = carry
        key_block = lax.dynamic_slice_in_dim(keys_all, index * span_rows, span_rows, 0)
        value_block = lax.dynamic_slice_in_dim(values_all, index * span_rows, span_rows, 0)
        scores = (
            jnp.einsum("qkgd,nkd->kgqn", query_b, key_block, preferred_element_type=jnp.float32)
            * scale
        )
        key_index = index * span_rows + jnp.arange(span_rows)
        allowed = key_index[None, :] <= query_index[:, None]
        probs = jnp.where(allowed, jnp.exp(scores - logsum[..., None]), 0.0)
        value_part = jnp.einsum(
            "kgqn,qkgd->nkd", probs.astype(jnp.bfloat16), back_b, preferred_element_type=jnp.float32
        )
        slopes = jnp.einsum(
            "qkgd,nkd->kgqn", back_b, value_block, preferred_element_type=jnp.float32
        )
        score_back = (probs * (slopes - delta[..., None])).astype(jnp.bfloat16)
        query_back = (
            query_back
            + jnp.einsum(
                "kgqn,nkd->qkgd", score_back, key_block, preferred_element_type=jnp.float32
            )
            * scale
        )
        key_part = (
            jnp.einsum("kgqn,qkgd->nkd", score_back, query_b, preferred_element_type=jnp.float32)
            * scale
        )
        key_buffer = lax.dynamic_update_slice_in_dim(key_buffer, key_part, index * span_rows, 0)
        value_buffer = lax.dynamic_update_slice_in_dim(
            value_buffer, value_part, index * span_rows, 0
        )
        return (query_back, key_buffer, value_buffer)

    init = (
        jnp.zeros(query_b.shape, jnp.float32),
        jnp.zeros(keys_all.shape, jnp.float32),
        jnp.zeros(values_all.shape, jnp.float32),
    )
    return lax.fori_loop(0, first_query // span_rows + 1, block, init)


def per_device(
    tokens,
    positions,
    first_gain,
    query_weight,
    key_weight,
    value_weight,
    query_gain,
    key_gain,
    output_weight,
    second_gain,
    gate_weight,
    up_weight,
    down_weight,
    upstream,
):
    sequences, rows, width = tokens.shape
    span_rows = positions.shape[1]
    head_dim = query_gain.shape[0]
    first_query = lax.axis_index("ctx") * span_rows
    query_acc = jnp.zeros((width, query_weight.shape[1]), jnp.float32)
    key_acc = jnp.zeros((width, key_weight.shape[1]), jnp.float32)
    value_acc = jnp.zeros((width, value_weight.shape[1]), jnp.float32)
    output_acc = jnp.zeros((output_weight.shape[0], width), jnp.float32)
    gate_acc = jnp.zeros((width, gate_weight.shape[1]), jnp.float32)
    up_acc = jnp.zeros((width, up_weight.shape[1]), jnp.float32)
    down_acc = jnp.zeros((down_weight.shape[0], width), jnp.float32)
    first_gain_acc = jnp.zeros_like(first_gain)
    second_gain_acc = jnp.zeros_like(second_gain)
    query_gain_acc = jnp.zeros_like(query_gain)
    key_gain_acc = jnp.zeros_like(key_gain)
    results = []
    gradients = []
    for seq in range(sequences):
        current = fetch_weights(
            query_weight,
            key_weight,
            value_weight,
            output_weight,
            gate_weight,
            up_weight,
            down_weight,
        )
        query_full, key_full, value_full, output_full, gate_full, up_full, down_full = current
        token_rows = tokens[seq].astype(jnp.float32)
        first = norm_rows(token_rows, first_gain).astype(jnp.bfloat16)
        first_all = lax.all_gather(first, "tp", axis=0, tiled=True)
        cosine, sine = rotary_tables(positions[seq], head_dim)
        query_raw = jnp.dot(first_all, query_full, preferred_element_type=jnp.float32).reshape(
            span_rows, -1, head_dim
        )
        key_raw = jnp.dot(first_all, key_full, preferred_element_type=jnp.float32).reshape(
            span_rows, -1, head_dim
        )
        value_b = (
            jnp.dot(first_all, value_full, preferred_element_type=jnp.float32)
            .astype(jnp.bfloat16)
            .reshape(span_rows, -1, head_dim)
        )
        kv_heads = key_raw.shape[1]
        group = query_raw.shape[1] // kv_heads

        def query_shape(raw, gain):
            return shape_heads(raw, gain, cosine, sine)

        query_b = (
            query_shape(query_raw, query_gain)
            .astype(jnp.bfloat16)
            .reshape(span_rows, kv_heads, group, head_dim)
        )
        key_b = query_shape(key_raw, key_gain).astype(jnp.bfloat16)
        attention, logsum = attend(query_b, key_b, value_b, first_query)
        mixed_b = jnp.transpose(attention, (2, 0, 1, 3)).reshape(span_rows, -1).astype(jnp.bfloat16)
        attn_rows = lax.psum_scatter(
            project_rows(mixed_b, output_full).astype(jnp.bfloat16),
            "tp",
            scatter_dimension=0,
            tiled=True,
        ).astype(jnp.float32)
        middle = token_rows + attn_rows
        second = norm_rows(middle, second_gain).astype(jnp.bfloat16)
        second_all = lax.all_gather(second, "tp", axis=0, tiled=True)
        gate = jnp.dot(second_all, gate_full, preferred_element_type=jnp.float32)
        up = jnp.dot(second_all, up_full, preferred_element_type=jnp.float32)
        gate_sig = jax.nn.sigmoid(gate)
        swish = gate * gate_sig
        hidden_b = (swish * up).astype(jnp.bfloat16)
        ffn_rows = lax.psum_scatter(
            project_rows(hidden_b, down_full).astype(jnp.bfloat16),
            "tp",
            scatter_dimension=0,
            tiled=True,
        ).astype(jnp.float32)
        results.append((middle + ffn_rows).astype(jnp.bfloat16))
        current = fetch_weights(
            query_weight,
            key_weight,
            value_weight,
            output_weight,
            gate_weight,
            up_weight,
            down_weight,
        )
        query_full, key_full, value_full, output_full, gate_full, up_full, down_full = current
        upstream_b = upstream[seq]
        upstream_all = lax.all_gather(upstream_b, "tp", axis=0, tiled=True)
        down_acc = down_acc + dot_first(hidden_b, upstream_all)
        hidden_back = dot_last(upstream_all, down_full)
        gate_back = (hidden_back * up * (gate_sig * (1.0 + gate * (1.0 - gate_sig)))).astype(
            jnp.bfloat16
        )
        up_back = (hidden_back * swish).astype(jnp.bfloat16)
        gate_acc = gate_acc + dot_first(second_all, gate_back)
        up_acc = up_acc + dot_first(second_all, up_back)
        second_back = lax.psum_scatter(
            project_pair(gate_back, gate_full, up_back, up_full).astype(jnp.bfloat16),
            "tp",
            scatter_dimension=0,
            tiled=True,
        ).astype(jnp.float32)
        unused_second, second_fn = jax.vjp(norm_rows, middle, second_gain)
        middle_part, second_part = second_fn(second_back)
        second_gain_acc = second_gain_acc + second_part
        middle_back = upstream_b.astype(jnp.float32) + middle_part
        mixed_back_all = lax.all_gather(middle_back.astype(jnp.bfloat16), "tp", axis=0, tiled=True)
        output_acc = output_acc + dot_first(mixed_b, mixed_back_all)
        attention_back = (
            dot_last(mixed_back_all, output_full)
            .astype(jnp.bfloat16)
            .reshape(span_rows, kv_heads, group, head_dim)
        )
        keys_all, values_all = (
            lax.all_gather(key_b, "ctx", axis=0, tiled=True),
            lax.all_gather(value_b, "ctx", axis=0, tiled=True),
        )
        query_back, key_buffer, value_buffer = attend_back(
            query_b, keys_all, values_all, attention_back, attention, logsum, first_query
        )
        key_back, value_back = (
            lax.psum_scatter(
                key_buffer.astype(jnp.bfloat16), "ctx", scatter_dimension=0, tiled=True
            ).astype(jnp.float32),
            lax.psum_scatter(
                value_buffer.astype(jnp.bfloat16), "ctx", scatter_dimension=0, tiled=True
            ).astype(jnp.float32),
        )
        value_back_b = value_back.reshape(span_rows, -1).astype(jnp.bfloat16)
        unused_key, key_fn = jax.vjp(query_shape, key_raw, key_gain)
        key_raw_back, key_gain_part = key_fn(key_back)
        unused_query, query_fn = jax.vjp(query_shape, query_raw, query_gain)
        query_raw_back, query_gain_part = query_fn(query_back.reshape(span_rows, -1, head_dim))
        key_raw_b = key_raw_back.reshape(span_rows, -1).astype(jnp.bfloat16)
        query_raw_b = query_raw_back.reshape(span_rows, -1).astype(jnp.bfloat16)
        key_gain_acc = key_gain_acc + key_gain_part
        query_gain_acc = query_gain_acc + query_gain_part
        query_acc = query_acc + dot_first(first_all, query_raw_b)
        key_acc = key_acc + dot_first(first_all, key_raw_b)
        value_acc = value_acc + dot_first(first_all, value_back_b)
        first_back = lax.psum_scatter(
            project_three(
                query_raw_b, query_full, key_raw_b, key_full, value_back_b, value_full
            ).astype(jnp.bfloat16),
            "tp",
            scatter_dimension=0,
            tiled=True,
        ).astype(jnp.float32)
        unused_first, first_fn = jax.vjp(norm_rows, token_rows, first_gain)
        token_part, first_part = first_fn(first_back)
        first_gain_acc = first_gain_acc + first_part
        gradients.append(middle_back + token_part)
    query_out, key_out, value_out, output_out, gate_out, up_out, down_out = (
        lax.psum_scatter(query_acc, ("shard", "ctx"), scatter_dimension=0, tiled=True),
        lax.psum_scatter(key_acc, ("shard", "ctx"), scatter_dimension=0, tiled=True),
        lax.psum_scatter(value_acc, ("shard", "ctx"), scatter_dimension=0, tiled=True),
        lax.psum_scatter(output_acc, ("shard", "ctx"), scatter_dimension=1, tiled=True),
        lax.psum_scatter(gate_acc, ("shard", "ctx"), scatter_dimension=0, tiled=True),
        lax.psum_scatter(up_acc, ("shard", "ctx"), scatter_dimension=0, tiled=True),
        lax.psum_scatter(down_acc, ("shard", "ctx"), scatter_dimension=1, tiled=True),
    )
    first_total, second_total, query_total, key_total = lax.psum(
        (first_gain_acc, second_gain_acc, query_gain_acc, key_gain_acc), ("shard", "ctx", "tp")
    )
    return (
        jnp.stack(results),
        jnp.stack(gradients),
        query_out,
        key_out,
        value_out,
        output_out,
        gate_out,
        up_out,
        down_out,
        first_total,
        second_total,
        query_total,
        key_total,
    )


def solution(mesh):
    in_specs = (
        P("shard", ("ctx", "tp"), None),
        P("shard", "ctx"),
        P(),
        P(("shard", "ctx"), "tp"),
        P(("shard", "ctx"), "tp"),
        P(("shard", "ctx"), "tp"),
        P(),
        P(),
        P("tp", ("shard", "ctx")),
        P(),
        P(("shard", "ctx"), "tp"),
        P(("shard", "ctx"), "tp"),
        P("tp", ("shard", "ctx")),
        P("shard", ("ctx", "tp"), None),
    )
    out_specs = (
        P("shard", ("ctx", "tp"), None),
        P("shard", ("ctx", "tp"), None),
        P(("shard", "ctx"), "tp"),
        P(("shard", "ctx"), "tp"),
        P(("shard", "ctx"), "tp"),
        P("tp", ("shard", "ctx")),
        P(("shard", "ctx"), "tp"),
        P(("shard", "ctx"), "tp"),
        P("tp", ("shard", "ctx")),
        P(),
        P(),
        P(),
        P(),
    )
    return jax.shard_map(
        per_device, mesh=mesh, in_specs=in_specs, out_specs=out_specs, check_vma=False
    )
```

profile of v0, /device:TPU:0, one launch (start us, length us, event | category | flops | bytes accessed | tf_op | source)
XLA Modules:
  0.0 1653.8 jit_solution(1743868269783206539)
XLA Ops:
  14.1 10.8 all_gather.39
  26.7 35.4 %all-gather.18.cloned.1.call-done = bf16[1024,1024]{1,0:T(8,128)(2,1)} async-done(((bf16[256,1024]{1,0:T(8,128)(2,1)}), bf16[1024,1024]{1,0:T(8,128)(2,1)}) %all-gather.18.cloned.1.call-update) | async-done | bytes 2097168 | tf_op jit(solution)/shard_map/all_gather | solution.py:204
  65.1 43.7 %all-gather.32.cloned.1.call-done = bf16[1024,1024]{1,0:T(8,128)(2,1)} async-done(((bf16[256,1024]{1,0:T(8,128)(2,1)}), bf16[1024,1024]{1,0:T(8,128)(2,1)}) %all-gather.32.cloned.1.call-update) | async-done | bytes 2097168 | tf_op jit(solution)/shard_map/all_gather | solution.py:204
  114.0 9.6 all_gather.42
  125.2 10.8 all_gather.41
  140.3 12.0 all_gather.88
  164.3 84.7 %conditional.2 = (f32[2,2,1024]{2,1,0:T(2,128)}, f32[2,2,1024]{2,1,0:T(2,128)}, f32[2,2,1024,64]{2,3,1,0:T(8,128)S(1)}, f32[2,2,1024]{2,1,0:T(2,128)S(1)}) conditional(s32[]{:T(128)} %convert_element_type.260, () %tuple.36, (s32[1024]{0:T(1024)S(1)}, bf16[4096,2,64]{0,2,1:T(8,128)(2,1)}, bf16[1024,2,2,64]{0,3,2,1:T(8,128)(2,1)}, ...), branch_computations={%region_3.0_spmd, %region_4.7_spmd} | conditional | flops 4517261312 | bytes 226103360 | solution.py:105
  170.2 27.5 %fusion.4 = (f32[2,2,1024]{2,1,0:T(2,128)S(1)}, f32[2,4096,1024,2]{2,1,3,0:T(8,128)}) fusion(pred[1024,4096]{0,1:T(8,128)(4,1)} %iota_compare_fusion, bf16[1024,2,2,64]{0,3,2,1:T(8,128)(2,1)} %get-tuple-element.116, bf16[4096,2,64]{0,2,1:T(8,128)(2,1)} %get-tuple-element.115), kind=kOutput, calls=%fused_computation.4 | convolution fusion | flops 2197811200 | bytes 72892416 | tf_op jit(solution)/shard_map/cond/branch_1_fun/qkgd,nkd->kgqn/dot_general | solution.py:88
  198.3 23.9 %fusion.6 = f32[2,2,1024]{2,1,0:T(2,128)} fusion(f32[2,4096,1024,2]{2,1,3,0:T(8,128)} %get-tuple-element.326, f32[2,2,1024]{2,1,0:T(2,128)} %broadcast_maximum_fusion, pred[1024,4096]{0,1:T(8,128)(4,1)} %iota_compare_fusion), kind=kLoop, calls=%fused_computation.6 | loop fusion | flops 83881984 | bytes 71335936 | tf_op jit(solution)/shard_map/cond/branch_1_fun/reduce_sum | solution.py:96
  222.2 26.1 %fusion.7 = f32[2,2,1024,64]{2,3,1,0:T(8,128)S(1)} fusion(f32[2,4096,1024,2]{2,1,3,0:T(8,128)} %get-tuple-element.326, f32[2,2,1024]{2,1,0:T(2,128)} %broadcast_maximum_fusion, pred[1024,4096]{0,1:T(8,128)(4,1)} %iota_compare_fusion, bf16[4096,2,64]{0,2,1:T(8,128)(2,1)S(1)} %copy-done.129), kind=kOutput, calls=%fused_computation.7 | convolution fusion | flops 2231369728 | bytes 73416704 | tf_op jit(solution)/shard_map/cond/branch_1_fun/kgqn,nkd->kgqd/dot_general | solution.py:97
  252.9 83.4 %conditional.3 = (f32[2,2,1024]{2,1,0:T(2,128)}, f32[2,2,1024]{2,1,0:T(2,128)}, f32[2,2,1024,64]{2,3,1,0:T(8,128)S(1)}, f32[2,2,1024]{2,1,0:T(2,128)S(1)}) conditional(s32[]{:T(128)} %convert_element_type.260, () %tuple.38, (s32[1024]{0:T(1024)S(1)}, bf16[4096,2,64]{0,2,1:T(8,128)(2,1)}, bf16[1024,2,2,64]{0,3,2,1:T(8,128)(2,1)S(1)}, ...), branch_computations={%region_13.14_spmd, %region_14.17_spmd} | conditional | flops 4517261312 | bytes 230297696 | solution.py:105
  258.8 25.9 %fusion.16 = (f32[2,2,1024]{2,1,0:T(2,128)S(1)}, f32[2,4096,1024,2]{2,1,3,0:T(8,128)}) fusion(pred[1024,4096]{0,1:T(8,128)(4,1)} %iota_compare_fusion.1, bf16[1024,2,2,64]{0,3,2,1:T(8,128)(2,1)S(1)} %get-tuple-element.120, bf16[4096,2,64]{0,2,1:T(8,128)(2,1)S(1)} %copy-done.37), kind=kOutput, calls=%fused_computation.19 | convolution fusion | flops 2197811200 | bytes 72892416 | tf_op jit(solution)/shard_map/cond/branch_1_fun/qkgd,nkd->kgqn/dot_general | solution.py:88
  285.4 24.1 %fusion.18 = f32[2,2,1024]{2,1,0:T(2,128)} fusion(f32[2,4096,1024,2]{2,1,3,0:T(8,128)} %get-tuple-element.328, f32[2,2,1024]{2,1,0:T(2,128)} %broadcast_maximum_fusion.1, pred[1024,4096]{0,1:T(8,128)(4,1)} %iota_compare_fusion.1), kind=kLoop, calls=%fused_computation.21 | loop fusion | flops 83881984 | bytes 71335936 | tf_op jit(solution)/shard_map/cond/branch_1_fun/reduce_sum | solution.py:96
  309.4 26.1 %fusion.19 = f32[2,2,1024,64]{2,3,1,0:T(8,128)S(1)} fusion(f32[2,4096,1024,2]{2,1,3,0:T(8,128)} %get-tuple-element.328, f32[2,2,1024]{2,1,0:T(2,128)} %broadcast_maximum_fusion.1, pred[1024,4096]{0,1:T(8,128)(4,1)} %iota_compare_fusion.1, bf16[4096,2,64]{0,2,1:T(8,128)(2,1)S(1)} %copy-done.128), kind=kOutput, calls=%fused_computation.22 | convolution fusion | flops 2231369728 | bytes 73416704 | tf_op jit(solution)/shard_map/cond/branch_1_fun/kgqn,nkd->kgqd/dot_general | solution.py:97
  340.0 42.3 %reduce-scatter.24.cloned.1.call-done = bf16[256,1024]{1,0:T(8,128)(2,1)} async-done(((bf16[1024,1024]{1,0:T(8,128)(2,1)}), bf16[256,1024]{1,0:T(8,128)(2,1)}) %reduce-scatter.24.cloned.1.call-update) | async-done | bytes 524304 | tf_op jit(solution)/shard_map/reduce_scatter | solution.py:231
  391.0 40.7 %all-gather.24.cloned.1.call-done = bf16[1024,1024]{1,0:T(8,128)(2,1)} async-done(((bf16[256,1024]{1,0:T(8,128)(2,1)}), bf16[1024,1024]{1,0:T(8,128)(2,1)}) %all-gather.24.cloned.1.call-update) | async-done | bytes 2097168 | tf_op jit(solution)/shard_map/all_gather | solution.py:239
  439.1 22.1 %all-gather.28.cloned.1.call-done = bf16[1024,1152]{1,0:T(8,128)(2,1)} async-done(((bf16[128,1152]{1,0:T(8,128)(2,1)}), bf16[1024,1152]{1,0:T(8,128)(2,1)}) %all-gather.28.cloned.1.call-update) | async-done | bytes 2359312 | tf_op jit(solution)/shard_map/all_gather | solution.py:67
  468.6 40.3 %all-gather.44.cloned.1.call-done = bf16[1,1024,1024]{2,1,0:T(8,128)(2,1)} async-done(((bf16[1,256,1024]{2,1,0:T(8,128)(2,1)}), bf16[1,1024,1024]{2,1,0:T(8,128)(2,1)}) %all-gather.44.cloned.1.call-update) | async-done | bytes 2097168 | tf_op jit(solution)/shard_map/all_gather | solution.py:263
  508.9 29.9 %all-gather.30.cloned.1.call-done = bf16[1152,1024]{1,0:T(8,128)(2,1)} async-done(((bf16[1152,128]{1,0:T(8,128)(2,1)}), bf16[1152,1024]{1,0:T(8,128)(2,1)}) %all-gather.30.cloned.1.call-update) | async-done | bytes 2359312 | tf_op jit(solution)/shard_map/all_gather | solution.py:68
  538.8 10.8 multiply_convert_fusion.2
  557.4 49.3 %all-gather.38.cloned.1.call-done = bf16[1024,1024]{1,0:T(8,128)(2,1)} async-done(((bf16[256,1024]{1,0:T(8,128)(2,1)}), bf16[1024,1024]{1,0:T(8,128)(2,1)}) %all-gather.38.cloned.1.call-update) | async-done | bytes 2097168 | tf_op jit(solution)/shard_map/all_gather | solution.py:239
  618.6 36.3 %all-gather.46.cloned.1.call-done = bf16[1,1024,1024]{2,1,0:T(8,128)(2,1)} async-done(((bf16[1,256,1024]{2,1,0:T(8,128)(2,1)}), bf16[1,1024,1024]{2,1,0:T(8,128)(2,1)}) %all-gather.46.cloned.1.call-update) | async-done | bytes 2097168 | tf_op jit(solution)/shard_map/all_gather | solution.py:263
  654.9 10.9 multiply_convert_fusion
  680.7 35.6 %reduce-scatter.36.cloned.1.call-done = bf16[256,1024]{1,0:T(8,128)(2,1)} async-done(((bf16[1024,1024]{1,0:T(8,128)(2,1)}), bf16[256,1024]{1,0:T(8,128)(2,1)}) %reduce-scatter.36.cloned.1.call-update) | async-done | bytes 524304 | tf_op jit(solution)/shard_map/reduce_scatter | solution.py:272
  719.1 42.7 %reduce-scatter.26.cloned.1.call-done = bf16[256,1024]{1,0:T(8,128)(2,1)} async-done(((bf16[1024,1024]{1,0:T(8,128)(2,1)}), bf16[256,1024]{1,0:T(8,128)(2,1)}) %reduce-scatter.26.cloned.1.call-update) | async-done | bytes 524304 | tf_op jit(solution)/shard_map/reduce_scatter | solution.py:245
  767.1 43.3 %all-gather.40.cloned.1.call-done = bf16[1024,1024]{1,0:T(8,128)(2,1)} async-done(((bf16[256,1024]{1,0:T(8,128)(2,1)}), bf16[1024,1024]{1,0:T(8,128)(2,1)}) %all-gather.40.cloned.1.call-update) | async-done | bytes 2097168 | tf_op jit(solution)/shard_map/all_gather | solution.py:282
  815.4 35.1 %while.30 = (s32[]{:T(128)}, f32[1024,2,2,64]{0,3,2,1:T(8,128)S(1)}, bf16[4096,2,64]{0,2,1:T(8,128)(2,1)}, bf16[4096,2,64]{0,2,1:T(8,128)(2,1)}, s32[]{:T(128)},...) while((s32[]{:T(128)}, ...), condition=%wide.region_23.24_spmd.clone, body=%wide.region_22.23_spmd.clone.sunk | while | flops 2728003584 | bytes 93126936 | solution.py:155
  815.4 9.3 fusion.318
  825.4 9.2 fusion.319
  842.1 8.4 fusion.322
  862.6 34.7 %while.31 = (s32[]{:T(128)}, f32[1024,2,2,64]{0,3,2,1:T(8,128)S(1)}, bf16[4096,2,64]{0,2,1:T(8,128)(2,1)}, bf16[4096,2,64]{0,2,1:T(8,128)(2,1)}, s32[]{:T(128)},...) while((s32[]{:T(128)}, ...), condition=%wide.region_33.34_spmd.clone, body=%wide.region_32.33_spmd.clone.sunk | while | flops 2728003584 | bytes 99418456 | solution.py:155
  862.8 9.2 fusion.333
  872.7 9.5 fusion.334
  888.7 8.6 fusion.337
  910.4 68.9 %reduce-scatter.30.cloned.1.call-done = bf16[1024,2,64]{0,2,1:T(8,128)(2,1)} async-done(((bf16[4096,2,64]{0,2,1:T(8,128)(2,1)}), bf16[1024,2,64]{0,2,1:T(8,128)(2,1)}) %reduce-scatter.30.cloned.1.call-update) | async-done | bytes 262160 | tf_op jit(solution)/shard_map/reduce_scatter | solution.py:297
  980.5 142.9 %reduce-scatter.38.cloned.1.call-done = bf16[1024,2,64]{0,2,1:T(8,128)(2,1)} async-done(((bf16[4096,2,64]{0,2,1:T(8,128)(2,1)}), bf16[1024,2,64]{0,2,1:T(8,128)(2,1)}) %reduce-scatter.38.cloned.1.call-update) | async-done | bytes 262160 | tf_op jit(solution)/shard_map/reduce_scatter | solution.py:297
  1130.6 20.8 %reduce-scatter.32.cloned.1.call-done = bf16[1024,2,64]{0,2,1:T(8,128)(2,1)} async-done(((bf16[4096,2,64]{0,2,1:T(8,128)(2,1)}), bf16[1024,2,64]{0,2,1:T(8,128)(2,1)}) %reduce-scatter.32.cloned.1.call-update) | async-done | bytes 262160 | tf_op jit(solution)/shard_map/reduce_scatter | solution.py:300
  1162.8 16.0 reduce-scatter.40.cloned.1.call-done
  1238.9 31.9 %reduce-scatter.42.cloned.1.call-done = bf16[256,1024]{1,0:T(8,128)(2,1)} async-done(((bf16[1024,1024]{1,0:T(8,128)(2,1)}), bf16[256,1024]{1,0:T(8,128)(2,1)}) %reduce-scatter.42.cloned.1.call-update) | async-done | bytes 524304 | tf_op jit(solution)/shard_map/reduce_scatter | solution.py:316
  1273.0 43.3 %reduce-scatter.22.cloned.1.call-done = bf16[256,1024]{1,0:T(8,128)(2,1)} async-done(((bf16[1024,1024]{1,0:T(8,128)(2,1)}), bf16[256,1024]{1,0:T(8,128)(2,1)}) %reduce-scatter.22.cloned.1.call-update) | async-done | bytes 524304 | tf_op jit(solution)/shard_map/reduce_scatter | solution.py:245
  1319.6 39.9 %all-reduce.8 = (f32[1024]{0:T(1024)}, f32[1024]{0:T(1024)}, f32[64]{0:T(128)}, f32[64]{0:T(128)}) all-reduce(f32[1024]{0:T(1024)S(1)} %add.369, f32[1024]{0:T(1024)S(1)} %add.370, f32[64]{0:T(128)S(1)} %add.371, f32[64]{0:T(128)S(1)} %add.372), channel_id=1, replica_groups=mesh['shard'=2,'ctx'=4,'tp'=4] {'shard','ctx','tp'}, use_global_device_ids=true, to_apply=%region_49.50 | all-reduce | flops 2176 | bytes 17408 | tf_op jit(solution)/shard_map/psum | solution.py:337
  1365.2 9.0 reduce-scatter.52.cloned.1.call-done
  1374.2 58.2 %reduce-scatter.54.cloned.1.call-done = f32[128,1152]{1,0:T(8,128)} async-done(((f32[1024,1152]{1,0:T(8,128)}), f32[128,1152]{1,0:T(8,128)}) %reduce-scatter.54.cloned.1.call-update) | async-done | bytes 589840 | tf_op jit(solution)/shard_map/reduce_scatter | solution.py:334
  1432.3 57.9 %reduce-scatter.56.cloned.1.call-done = f32[1152,128]{1,0:T(8,128)} async-done(((f32[1152,1024]{1,0:T(8,128)}), f32[1152,128]{1,0:T(8,128)}) %reduce-scatter.56.cloned.1.call-update) | async-done | bytes 589840 | tf_op jit(solution)/shard_map/reduce_scatter | solution.py:335
  1490.3 40.1 %reduce-scatter.44.cloned.1.call-done = f32[128,256]{1,0:T(8,128)} async-done(((f32[1024,256]{1,0:T(8,128)}), f32[128,256]{1,0:T(8,128)}) %reduce-scatter.44.cloned.1.call-update) | async-done | bytes 131088 | tf_op jit(solution)/shard_map/reduce_scatter | solution.py:329
  1530.4 40.1 %reduce-scatter.50.cloned.1.call-done = f32[256,128]{1,0:T(8,128)} async-done(((f32[256,1024]{1,0:T(8,128)}), f32[256,128]{1,0:T(8,128)}) %reduce-scatter.50.cloned.1.call-update) | async-done | bytes 131088 | tf_op jit(solution)/shard_map/reduce_scatter | solution.py:332
  1570.5 37.9 %reduce-scatter.46.cloned.1.call-done = f32[128,128]{1,0:T(8,128)} async-done(((f32[1024,128]{1,0:T(8,128)}), f32[128,128]{1,0:T(8,128)}) %reduce-scatter.46.cloned.1.call-update) | async-done | bytes 65552 | tf_op jit(solution)/shard_map/reduce_scatter | solution.py:330
  1608.5 37.7 %reduce-scatter.48.cloned.1.call-done = f32[128,128]{1,0:T(8,128)} async-done(((f32[1024,128]{1,0:T(8,128)}), f32[128,128]{1,0:T(8,128)}) %reduce-scatter.48.cloned.1.call-update) | async-done | bytes 65552 | tf_op jit(solution)/shard_map/reduce_scatter | solution.py:331
  (477 shorter events, 256.3 us)
Async XLA Ops:
  8.0 54.0 %all-gather.18.cloned.1.call-start = ((), (), s32[]{:S(2)}) async-start(), calls=%async_computation.19 | async-start | bytes 2621440 | tf_op jit(solution)/shard_map/all_gather | solution.py:204
  13.3 95.5 %all-gather.32.cloned.1.call-start = ((), (), s32[]{:S(2)}) async-start(), calls=%async_computation.28 | async-start | bytes 2621440 | tf_op jit(solution)/shard_map/all_gather | solution.py:204
  14.0 150.3 %all-gather.20.cloned.1.call-start = ((), (), s32[]{:S(2)}) async-start(), calls=%async_computation.20 | async-start | bytes 1310720 | tf_op jit(solution)/shard_map/all_gather | solution.py:82
  113.9 50.4 %all-gather.22.cloned.1.call-start = ((), (), s32[]{:S(2)}) async-start(), calls=%async_computation.21 | async-start | bytes 1310720 | tf_op jit(solution)/shard_map/all_gather | solution.py:83
  125.2 127.7 %all-gather.34.cloned.1.call-start = ((), (), s32[]{:S(2)}) async-start(), calls=%async_computation.29 | async-start | bytes 1310720 | tf_op jit(solution)/shard_map/all_gather | solution.py:82
  140.2 112.7 %all-gather.36.cloned.1.call-start = ((), (), s32[]{:S(2)}) async-start(), calls=%async_computation.30 | async-start | bytes 1310720 | tf_op jit(solution)/shard_map/all_gather | solution.py:83
  156.7 183.3 %reduce-scatter.20.cloned.1.call-start = ((), (), s32[]{:S(2)}) async-start(), calls=%async_computation.22 | async-start | bytes 2621440 | tf_op jit(solution)/shard_map/reduce_scatter | solution.py:231
  252.6 129.7 %reduce-scatter.24.cloned.1.call-start = ((), (), s32[]{:S(2)}) async-start(), calls=%async_computation.31 | async-start | bytes 2621440 | tf_op jit(solution)/shard_map/reduce_scatter | solution.py:231
  339.4 51.6 %all-gather.26.cloned.1.call-start = ((), (), s32[]{:S(2)}) async-start(), calls=%async_computation.24 | async-start | bytes 2654208 | tf_op jit(solution)/shard_map/all_gather | solution.py:66
  340.0 91.8 %all-gather.24.cloned.1.call-start = ((), (), s32[]{:S(2)}) async-start(), calls=%async_computation.23 | async-start | bytes 2621440 | tf_op jit(solution)/shard_map/all_gather | solution.py:239
  384.0 377.8 %copy-start.96 = (f32[256]{0:T(256)}, f32[256]{0:T(256)S(1)}, u32[]{:S(2)}) copy-start(f32[256]{0:T(256)S(1)} %fusion.156) | copy-start | bytes 3076
  384.0 377.8 %copy-start.94 = (f32[256]{0:T(256)}, f32[256]{0:T(256)S(1)}, u32[]{:S(2)}) copy-start(f32[256]{0:T(256)S(1)} %fusion.158) | copy-start | bytes 3076
  386.7 74.4 %all-gather.28.cloned.1.call-start = ((), (), s32[]{:S(2)}) async-start(), calls=%async_computation.25 | async-start | bytes 2654208 | tf_op jit(solution)/shard_map/all_gather | solution.py:67
  387.3 121.6 %all-gather.44.cloned.1.call-start = ((), (), s32[]{:S(2)}) async-start(), calls=%async_computation.51 | async-start | bytes 2621440 | tf_op jit(solution)/shard_map/all_gather | solution.py:263
  388.4 150.4 %all-gather.30.cloned.1.call-start = ((), (), s32[]{:S(2)}) async-start(), calls=%async_computation.26 | async-start | bytes 2654208 | tf_op jit(solution)/shard_map/all_gather | solution.py:68
  389.2 217.5 %all-gather.38.cloned.1.call-start = ((), (), s32[]{:S(2)}) async-start(), calls=%async_computation.32 | async-start | bytes 2621440 | tf_op jit(solution)/shard_map/all_gather | solution.py:239
  389.9 265.0 %all-gather.46.cloned.1.call-start = ((), (), s32[]{:S(2)}) async-start(), calls=%async_computation.52 | async-start | bytes 2621440 | tf_op jit(solution)/shard_map/all_gather | solution.py:263
  390.5 290.2 %reduce-scatter.28.cloned.1.call-start = ((), (), s32[]{:S(2)}) async-start(), calls=%async_computation.34 | async-start | bytes 2621440 | tf_op jit(solution)/shard_map/reduce_scatter | solution.py:272
  557.1 159.1 %reduce-scatter.36.cloned.1.call-start = ((), (), s32[]{:S(2)}) async-start(), calls=%async_computation.39 | async-start | bytes 2621440 | tf_op jit(solution)/shard_map/reduce_scatter | solution.py:272
  673.4 88.4 %reduce-scatter.26.cloned.1.call-start = ((), (), s32[]{:S(2)}) async-start(), calls=%async_computation.33 | async-start | bytes 2621440 | tf_op jit(solution)/shard_map/reduce_scatter | solution.py:245
  680.2 130.2 %all-gather.40.cloned.1.call-start = ((), (), s32[]{:S(2)}) async-start(), calls=%async_computation.35 | async-start | bytes 2621440 | tf_op jit(solution)/shard_map/all_gather | solution.py:282
  765.4 91.4 %all-gather.42.cloned.1.call-start = ((), (), s32[]{:S(2)}) async-start(), calls=%async_computation.40 | async-start | bytes 2621440 | tf_op jit(solution)/shard_map/all_gather | solution.py:282
  767.0 212.3 %reduce-scatter.30.cloned.1.call-start = ((), (), s32[]{:S(2)}) async-start(), calls=%async_computation.36 | async-start | bytes 1310720 | tf_op jit(solution)/shard_map/reduce_scatter | solution.py:297
  850.6 272.8 %reduce-scatter.38.cloned.1.call-start = ((), (), s32[]{:S(2)}) async-start(), calls=%async_computation.41 | async-start | bytes 1310720 | tf_op jit(solution)/shard_map/reduce_scatter | solution.py:297
  897.3 254.2 %reduce-scatter.32.cloned.1.call-start = ((), (), s32[]{:S(2)}) async-start(), calls=%async_computation.37 | async-start | bytes 1310720 | tf_op jit(solution)/shard_map/reduce_scatter | solution.py:300
  900.8 278.0 %reduce-scatter.40.cloned.1.call-start = ((), (), s32[]{:S(2)}) async-start(), calls=%async_computation.42 | async-start | bytes 1310720 | tf_op jit(solution)/shard_map/reduce_scatter | solution.py:300
  907.5 215.9 %copy-start.46 = (f32[1024,64]{0,1:T(8,128)S(1)}, f32[1024,64]{0,1:T(8,128)}, u32[]{:S(2)}) copy-start(f32[1024,64]{0,1:T(8,128)} %copy-done.45) | copy-start | bytes 786436
  907.5 217.1 %copy-start.18 = (f32[1024,128]{0,1:T(8,128)S(1)}, f32[1024,128]{0,1:T(8,128)}, u32[]{:S(2)}) copy-start(f32[1024,128]{0,1:T(8,128)} %copy-done.17) | copy-start | bytes 1572868
  907.5 217.1 %copy-start.20 = (f32[1024,128]{0,1:T(8,128)S(1)}, f32[1024,128]{0,1:T(8,128)}, u32[]{:S(2)}) copy-start(f32[1024,128]{0,1:T(8,128)} %copy-done.19) | copy-start | bytes 1572868
  907.5 217.1 %copy-start.31 = (f32[1024,64]{0,1:T(8,128)S(1)}, f32[1024,64]{0,1:T(8,128)}, u32[]{:S(2)}) copy-start(f32[1024,64]{0,1:T(8,128)} %copy-done.28) | copy-start | bytes 786436
  907.5 217.1 %copy-start.81 = (f32[1024,2]{0,1:T(2,128)S(1)}, f32[1024,2]{0,1:T(2,128)}, u32[]{:S(2)}) copy-start(f32[1024,2]{0,1:T(2,128)} %copy-done.80) | copy-start | bytes 24580
  907.5 217.1 %copy-start.83 = (f32[1024,2]{0,1:T(2,128)S(1)}, f32[1024,2]{0,1:T(2,128)}, u32[]{:S(2)}) copy-start(f32[1024,2]{0,1:T(2,128)} %copy-done.82) | copy-start | bytes 24580
  907.5 217.1 %copy-start.116 = (f32[64]{0:T(128)S(1)}, f32[64]{0:T(128)}, u32[]{:S(2)}) copy-start(f32[64]{0:T(128)} %param.29) | copy-start | bytes 772
  910.4 215.8 %copy-start.87 = (f32[1024,2]{0,1:T(2,128)S(1)}, f32[1024,2]{0,1:T(2,128)}, u32[]{:S(2)}) copy-start(f32[1024,2]{0,1:T(2,128)} %copy-done.86) | copy-start | bytes 24580
  910.4 215.9 %copy-start.89 = (f32[1024,2]{0,1:T(2,128)S(1)}, f32[1024,2]{0,1:T(2,128)}, u32[]{:S(2)}) copy-start(f32[1024,2]{0,1:T(2,128)} %copy-done.88) | copy-start | bytes 24580
  910.4 328.5 %reduce-scatter.34.cloned.1.call-start = ((), (), s32[]{:S(2)}) async-start(), calls=%async_computation.38 | async-start | bytes 2621440 | tf_op jit(solution)/shard_map/reduce_scatter | solution.py:316
  979.4 145.3 %copy-start.65 = (bf16[1024,2,64]{0,2,1:T(8,128)(2,1)S(1)}, bf16[1024,2,64]{0,2,1:T(8,128)(2,1)}, u32[]{:S(2)}) copy-start(bf16[1024,2,64]{0,2,1:T(8,128)(2,1)} %reduce-scatter.30.cloned.1.call-done) | copy-start | bytes 786436
  980.5 145.8 %copy-start.67 = (f32[1024,2,32]{0,2,1:T(8,128)}, f32[1024,2,32]{0,2,1:T(8,128)S(1)}, u32[]{:S(2)}) copy-start(f32[1024,2,32]{0,2,1:T(8,128)S(1)} %get-tuple-element.358) | copy-start | bytes 786436
  980.5 145.8 %copy-start.68 = (f32[1024,2,32]{0,2,1:T(8,128)}, f32[1024,2,32]{0,2,1:T(8,128)S(1)}, u32[]{:S(2)}) copy-start(f32[1024,2,32]{0,2,1:T(8,128)S(1)} %get-tuple-element.359) | copy-start | bytes 786436
  1157.2 113.7 %reduce-scatter.42.cloned.1.call-start = ((), (), s32[]{:S(2)}) async-start(), calls=%async_computation.43 | async-start | bytes 2621440 | tf_op jit(solution)/shard_map/reduce_scatter | solution.py:316
  1184.4 131.9 %reduce-scatter.22.cloned.1.call-start = ((), (), s32[]{:S(2)}) async-start(), calls=%async_computation.27 | async-start | bytes 2621440 | tf_op jit(solution)/shard_map/reduce_scatter | solution.py:245
  1191.2 183.0 %reduce-scatter.52.cloned.1.call-start = ((), (), s32[]{:S(2)}) async-start(), calls=%async_computation.48 | async-start | bytes 5308416 | tf_op jit(solution)/shard_map/reduce_scatter | solution.py:333
  1201.3 231.0 %reduce-scatter.54.cloned.1.call-start = ((), (), s32[]{:S(2)}) async-start(), calls=%async_computation.49 | async-start | bytes 5308416 | tf_op jit(solution)/shard_map/reduce_scatter | solution.py:334
  1211.0 279.3 %reduce-scatter.56.cloned.1.call-start = ((), (), s32[]{:S(2)}) async-start(), calls=%async_computation.50 | async-start | bytes 5308416 | tf_op jit(solution)/shard_map/reduce_scatter | solution.py:335
  1221.4 309.0 %reduce-scatter.44.cloned.1.call-start = ((), (), s32[]{:S(2)}) async-start(), calls=%async_computation.44 | async-start | bytes 1179648 | tf_op jit(solution)/shard_map/reduce_scatter | solution.py:329
  1227.6 342.9 %reduce-scatter.50.cloned.1.call-start = ((), (), s32[]{:S(2)}) async-start(), calls=%async_computation.47 | async-start | bytes 1179648 | tf_op jit(solution)/shard_map/reduce_scatter | solution.py:332
  1231.9 376.6 %reduce-scatter.46.cloned.1.call-start = ((), (), s32[]{:S(2)}) async-start(), calls=%async_computation.45 | async-start | bytes 589824 | tf_op jit(solution)/shard_map/reduce_scatter | solution.py:330
  1235.5 410.7 %reduce-scatter.48.cloned.1.call-start = ((), (), s32[]{:S(2)}) async-start(), calls=%async_computation.46 | async-start | bytes 589824 | tf_op jit(solution)/shard_map/reduce_scatter | solution.py:331
  (123 other events, 2753.7 us)
Sparse Core Ops, SparseCore 0:
  13.4 48.6 all-gather.17
  64.2 44.5 all-gather.31
  114.1 15.5 all-gather.19
  131.7 17.8 all-gather.21
  151.0 17.9 all-gather.33
  170.4 16.7 all-gather.35
  252.7 42.6 reduce-scatter.19
  339.5 42.7 reduce-scatter.23
  557.2 63.3 reduce-scatter.27
  673.6 42.6 reduce-scatter.35
  718.6 43.1 reduce-scatter.25
  850.7 128.6 reduce-scatter.29
  981.9 141.4 reduce-scatter.37
  1126.5 24.8 reduce-scatter.31
  1153.8 24.8 reduce-scatter.39
  1181.6 43.8 reduce-scatter.33
  1227.6 43.1 reduce-scatter.41
  1273.1 43.1 reduce-scatter.21
  1320.3 53.8 reduce-scatter.51
  1378.4 53.8 reduce-scatter.53
  1436.4 53.8 reduce-scatter.55
  1494.3 36.0 reduce-scatter.43
  1534.5 35.9 reduce-scatter.49
  1574.3 34.0 reduce-scatter.45
  1612.1 34.0 reduce-scatter.47
Sparse Core Ops, SparseCore 1:
  341.7 27.7 all-gather.25
  386.8 44.9 all-gather.23
  433.5 27.6 all-gather.27
  463.3 45.5 all-gather.43
  510.8 28.0 all-gather.29
  541.1 65.5 all-gather.37
  608.1 46.7 all-gather.45
  765.5 44.8 all-gather.39
  812.4 44.3 all-gather.41
where the time goes:
time: 1660 us; the launch traced here: 1650 us
  waiting for transfers between devices  1080 us (65%)
  matrix products  331 us (20%)
  other arithmetic  120 us (7%)
  blocking collectives  83.1 us (5%)
  local copies, waits for them, and re-layouts  20 us (1%)
  between operations  17.8 us (1%)
    reduce_scatter x2, waiting for transfers between devices, per_device(): lax.psum_scatter(key_buffer.astype(jnp.bfloat16), 'ctx', scatter_dimensio...  212 us
    all_gather x2, waiting for transfers between devices, per_device(): second_all = lax.all_gather(second, 'tp', axis=0, tiled=True)  90 us
    reduce_scatter x2, waiting for transfers between devices, per_device(): lax.psum_scatter(project_rows(hidden_b, down_full).astype(jnp.bfloat16),...  86 us
    all_gather x2, waiting for transfers between devices, per_device(): first_all = lax.all_gather(first, 'tp', axis=0, tiled=True)  79.1 us
    all_gather x2, waiting for transfers between devices, per_device(): upstream_all = lax.all_gather(upstream_b, 'tp', axis=0, tiled=True)  76.7 us
    dot_general x14, matrix products, dot_last(): lax.dot_general(left, right, (((1,), (1,)), ((), ())), preferred_element_...  64.4 us
    reduce_scatter x1, waiting for transfers between devices, per_device(): lax.psum_scatter(up_acc, ('shard', 'ctx'), scatter_dimension=0, tiled=True)  58.2 us
    reduce_scatter x1, waiting for transfers between devices, per_device(): lax.psum_scatter(down_acc, ('shard', 'ctx'), scatter_dimension=1, tiled=T...  57.9 us
  transfers between devices with their start and end apart: 34, of which 26 were waited for; matrix products, arithmetic and copies ran while one was open for 27% of the time, Pallas kernels for 0%

commit v1 on v0

--- a/solution.py
+++ b/solution.py
@@ -236,7 +236,22 @@
         ).astype(jnp.float32)
         middle = token_rows + attn_rows
         second = norm_rows(middle, second_gain).astype(jnp.bfloat16)
-        second_all = lax.all_gather(second, "tp", axis=0, tiled=True)
+
+        def _expand_runs(local_array):
+            mesh_name = "tp"
+            n_lanes = jax.lax.axis_size(mesh_name)
+            buffers = []
+            for k in range(n_lanes):
+                buffers.append((k, (k + 1) % n_lanes))
+            then = [None] * n_lanes
+            then[n_lanes - 1] = local_array
+            for dev in range(n_lanes - 2, -1, -1):
+                then[dev] = jax.lax.ppermute(then[dev + 1], mesh_name, buffers)
+            current_arr = jnp.concatenate(then, axis=0)
+            vec_out = jax.lax.axis_index(mesh_name)
+            return jnp.roll(current_arr, (vec_out + 1) * local_array.shape[0], axis=0)
+
+        second_all = _expand_runs(second)
         gate = jnp.dot(second_all, gate_full, preferred_element_type=jnp.float32)
         up = jnp.dot(second_all, up_full, preferred_element_type=jnp.float32)
         gate_sig = jax.nn.sigmoid(gate)

time: 1660 us -> 1630 us (0.982)
  waiting for transfers between devices: 1080 us -> 1030 us
    all_gather x2 -> x0, waiting for transfers between devices: 90 us -> none  [per_device(): second_all = lax.all_gather(second, 'tp', axis=0, tiled=True)]
    ppermute x0 -> x6, waiting for transfers between devices: none -> 56 us  [_expand_runs(): then[dev] = jax.lax.ppermute(then[dev + 1], mesh_name, buffers)]
    reduce_scatter x1, waiting for transfers between devices: 58.2 us -> 8.87 us  [per_device(): lax.psum_scatter(up_acc, ('shard', 'ctx'), scatter_dimension=0, tiled=True)]
    reduce_scatter x1, waiting for transfers between devices: 8.99 us -> 58.2 us  [per_device(): lax.psum_scatter(gate_acc, ('shard', 'ctx'), scatter_dimension=0, tiled=T...]
    all_gather x2, waiting for transfers between devices: 76.7 us -> 38.1 us  [per_device(): upstream_all = lax.all_gather(upstream_b, 'tp', axis=0, tiled=True)]
    all_gather x1, waiting for transfers between devices: 0.03 us -> 23.4 us  [fetch_weights(): lax.all_gather(gate_weight, ('shard', 'ctx'), axis=0, tiled=True)]
    concatenate x0 -> x2, other arithmetic: none -> 19.4 us  [_expand_runs(): return jnp.roll(current_arr, (vec_out + 1) * local_array.shape[0], axis=0)]
    reduce_scatter x2, waiting for transfers between devices: 35.6 us -> 52.4 us  [per_device(): lax.psum_scatter(project_pair(gate_back, gate_full, up_back, up_full).ast...]
  transfers between devices with their start and end apart: 34 -> 38, of which waited for: 26 -> 29; matrix products, arithmetic and copies ran while one was open for 27% -> 28% of each run, Pallas kernels for 0% -> 0%
where the time goes in v1:
time: 1630 us
  waiting for transfers between devices  1030 us (63%)
  matrix products  329 us (20%)
  other arithmetic  135 us (8%)
  blocking collectives  83.3 us (5%)
  starting transfers between devices  18.5 us (1%)
  local copies, waits for them, and re-layouts  16.3 us (1%)
    reduce_scatter x2, waiting for transfers between devices, per_device(): lax.psum_scatter(key_buffer.astype(jnp.bfloat16), 'ctx', scatter_dimensio...  206 us
    reduce_scatter x2, waiting for transfers between devices, per_device(): lax.psum_scatter(project_rows(hidden_b, down_full).astype(jnp.bfloat16),...  86 us
    all_gather x2, waiting for transfers between devices, per_device(): first_all = lax.all_gather(first, 'tp', axis=0, tiled=True)  80.4 us
    reduce_scatter x1, waiting for transfers between devices, per_device(): lax.psum_scatter(gate_acc, ('shard', 'ctx'), scatter_dimension=0, tiled=T...  58.2 us
    reduce_scatter x1, waiting for transfers between devices, per_device(): lax.psum_scatter(down_acc, ('shard', 'ctx'), scatter_dimension=1, tiled=T...  57.9 us
    ppermute x6, waiting for transfers between devices, _expand_runs(): then[dev] = jax.lax.ppermute(then[dev + 1], mesh_name, buffers)  56 us
    dot_general x14, matrix products, dot_last(): lax.dot_general(left, right, (((1,), (1,)), ((), ())), preferred_element_...  55.4 us
    dot_general x2, matrix products, update(): jnp.einsum('qkgd,nkd->kgqn', query_b, key_piece, preferred_element_type=j...  53.2 us
  transfers between devices with their start and end apart: 38, of which 29 were waited for; matrix products, arithmetic and copies ran while one was open for 28% of the time, Pallas kernels for 0%

profile of v1, /device:TPU:0, one launch (start us, length us, event | category | flops | bytes accessed | tf_op | source)
XLA Modules:
  0.0 1625.0 jit_solution(14618002352785917022)
XLA Ops:
  13.2 10.8 all_gather.35
  25.1 36.1 %all-gather.16.cloned.1.call-done = bf16[1024,1024]{1,0:T(8,128)(2,1)} async-done(((bf16[256,1024]{1,0:T(8,128)(2,1)}), bf16[1024,1024]{1,0:T(8,128)(2,1)}) %all-gather.16.cloned.1.call-update) | async-done | bytes 2097168 | tf_op jit(solution)/shard_map/all_gather | solution.py:204
  63.7 44.2 %all-gather.28.cloned.1.call-done = bf16[1024,1024]{1,0:T(8,128)(2,1)} async-done(((bf16[256,1024]{1,0:T(8,128)(2,1)}), bf16[1024,1024]{1,0:T(8,128)(2,1)}) %all-gather.28.cloned.1.call-update) | async-done | bytes 2097168 | tf_op jit(solution)/shard_map/all_gather | solution.py:204
  112.5 9.5 all_gather.38
  125.4 11.0 all_gather.37
  137.5 12.1 all_gather.40
  164.6 84.7 %conditional.3 = (f32[2,2,1024]{2,1,0:T(2,128)}, f32[2,2,1024]{2,1,0:T(2,128)}, f32[2,2,1024,64]{2,3,1,0:T(8,128)S(1)}, f32[2,2,1024]{2,1,0:T(2,128)S(1)}) conditional(s32[]{:T(128)} %convert_element_type.260, () %tuple.39, (s32[1024]{0:T(1024)S(1)}, bf16[4096,2,64]{0,2,1:T(8,128)(2,1)}, bf16[1024,2,2,64]{0,3,2,1:T(8,128)(2,1)}, ...), branch_computations={%region_13.15_spmd, %region_14.18_spmd} | conditional | flops 4517261312 | bytes 221909024 | solution.py:105
  170.4 27.3 %fusion.16 = (f32[2,2,1024]{2,1,0:T(2,128)S(1)}, f32[2,4096,1024,2]{2,1,3,0:T(8,128)}) fusion(pred[1024,4096]{0,1:T(8,128)(4,1)} %iota_compare_fusion.1, bf16[1024,2,2,64]{0,3,2,1:T(8,128)(2,1)} %get-tuple-element.121, bf16[4096,2,64]{0,2,1:T(8,128)(2,1)} %get-tuple-element.120), kind=kOutput, calls=%fused_computation.19 | convolution fusion | flops 2197811200 | bytes 72892416 | tf_op jit(solution)/shard_map/cond/branch_1_fun/qkgd,nkd->kgqn/dot_general | solution.py:88
  198.3 23.8 %fusion.18 = f32[2,2,1024]{2,1,0:T(2,128)} fusion(f32[2,4096,1024,2]{2,1,3,0:T(8,128)} %get-tuple-element.329, f32[2,2,1024]{2,1,0:T(2,128)} %broadcast_maximum_fusion.1, pred[1024,4096]{0,1:T(8,128)(4,1)} %iota_compare_fusion.1), kind=kLoop, calls=%fused_computation.21 | loop fusion | flops 83881984 | bytes 71335936 | tf_op jit(solution)/shard_map/cond/branch_1_fun/reduce_sum | solution.py:96
  222.9 26.4 %fusion.19 = f32[2,2,1024,64]{2,3,1,0:T(8,128)S(1)} fusion(f32[2,4096,1024,2]{2,1,3,0:T(8,128)} %get-tuple-element.329, f32[2,2,1024]{2,1,0:T(2,128)} %broadcast_maximum_fusion.1, pred[1024,4096]{0,1:T(8,128)(4,1)} %iota_compare_fusion.1, bf16[4096,2,64]{0,2,1:T(8,128)(2,1)} %get-tuple-element.122), kind=kOutput, calls=%fused_computation.22 | convolution fusion | flops 2231369728 | bytes 73416704 | tf_op jit(solution)/shard_map/cond/branch_1_fun/kgqn,nkd->kgqd/dot_general | solution.py:97
  253.2 83.4 %conditional.2 = (f32[2,2,1024]{2,1,0:T(2,128)}, f32[2,2,1024]{2,1,0:T(2,128)}, f32[2,2,1024,64]{2,3,1,0:T(8,128)S(1)}, f32[2,2,1024]{2,1,0:T(2,128)S(1)}) conditional(s32[]{:T(128)} %convert_element_type.260, () %tuple.37, (s32[1024]{0:T(1024)S(1)}, bf16[4096,2,64]{0,2,1:T(8,128)(2,1)}, bf16[1024,2,2,64]{0,3,2,1:T(8,128)(2,1)S(1)}, ...), branch_computations={%region_3.0_spmd, %region_4.7_spmd} | conditional | flops 4517261312 | bytes 230297696 | solution.py:105
  259.0 26.0 %fusion.4 = (f32[2,2,1024]{2,1,0:T(2,128)S(1)}, f32[2,4096,1024,2]{2,1,3,0:T(8,128)}) fusion(pred[1024,4096]{0,1:T(8,128)(4,1)} %iota_compare_fusion, bf16[1024,2,2,64]{0,3,2,1:T(8,128)(2,1)S(1)} %get-tuple-element.117, bf16[4096,2,64]{0,2,1:T(8,128)(2,1)S(1)} %copy-done.35), kind=kOutput, calls=%fused_computation.4 | convolution fusion | flops 2197811200 | bytes 72892416 | tf_op jit(solution)/shard_map/cond/branch_1_fun/qkgd,nkd->kgqn/dot_general | solution.py:88
  285.6 24.1 %fusion.6 = f32[2,2,1024]{2,1,0:T(2,128)} fusion(f32[2,4096,1024,2]{2,1,3,0:T(8,128)} %get-tuple-element.327, f32[2,2,1024]{2,1,0:T(2,128)} %broadcast_maximum_fusion, pred[1024,4096]{0,1:T(8,128)(4,1)} %iota_compare_fusion), kind=kLoop, calls=%fused_computation.6 | loop fusion | flops 83881984 | bytes 71335936 | tf_op jit(solution)/shard_map/cond/branch_1_fun/reduce_sum | solution.py:96
  310.4 26.2 %fusion.7 = f32[2,2,1024,64]{2,3,1,0:T(8,128)S(1)} fusion(f32[2,4096,1024,2]{2,1,3,0:T(8,128)} %get-tuple-element.327, f32[2,2,1024]{2,1,0:T(2,128)} %broadcast_maximum_fusion, pred[1024,4096]{0,1:T(8,128)(4,1)} %iota_compare_fusion, bf16[4096,2,64]{0,2,1:T(8,128)(2,1)S(1)} %copy-done.124), kind=kOutput, calls=%fused_computation.7 | convolution fusion | flops 2231369728 | bytes 73416704 | tf_op jit(solution)/shard_map/cond/branch_1_fun/kgqn,nkd->kgqd/dot_general | solution.py:97
  343.9 38.7 %reduce-scatter.20.cloned.1.call-done = bf16[256,1024]{1,0:T(8,128)(2,1)} async-done(((bf16[1024,1024]{1,0:T(8,128)(2,1)}), bf16[256,1024]{1,0:T(8,128)(2,1)}) %reduce-scatter.20.cloned.1.call-update) | async-done | bytes 524304 | tf_op jit(solution)/shard_map/reduce_scatter | solution.py:231
  388.2 20.6 %collective-permute-done.3 = bf16[256,1024]{1,0:T(8,128)(2,1)} collective-permute-done((bf16[256,1024]{1,0:T(8,128)(2,1)S(1)}, bf16[256,1024]{1,0:T(8,128)(2,1)}, u32[]{:S(2)}, u32[]{:S(2)}) %collective-permute-start.3) | collective-permute-done | bytes 524320 | tf_op jit(solution)/shard_map/ppermute | solution.py:249
  411.1 20.1 %collective-permute-done = bf16[256,1024]{1,0:T(8,128)(2,1)S(1)} collective-permute-done((bf16[256,1024]{1,0:T(8,128)(2,1)S(1)}, bf16[256,1024]{1,0:T(8,128)(2,1)S(1)}, u32[]{:S(2)}, u32[]{:S(2)}) %collective-permute-start) | collective-permute-done | bytes 524320 | tf_op jit(solution)/shard_map/ppermute | solution.py:249
  438.4 15.3 collective-permute-done.4
  464.2 29.4 %all-gather.26.cloned.1.call-done = bf16[1152,1024]{1,0:T(8,128)(2,1)} async-done(((bf16[1152,128]{1,0:T(8,128)(2,1)}), bf16[1152,1024]{1,0:T(8,128)(2,1)}) %all-gather.26.cloned.1.call-update) | async-done | bytes 2359312 | tf_op jit(solution)/shard_map/all_gather | solution.py:68
  502.8 9.3 fusion.95
  512.1 12.4 all-gather.24.cloned.1.call-done
  531.9 23.4 %all-gather.22.cloned.1.call-done = bf16[1024,1152]{1,0:T(8,128)(2,1)} async-done(((bf16[128,1152]{1,0:T(8,128)(2,1)}), bf16[1024,1152]{1,0:T(8,128)(2,1)}) %all-gather.22.cloned.1.call-update) | async-done | bytes 2359312 | tf_op jit(solution)/shard_map/all_gather | solution.py:66
  555.3 11.0 multiply_convert_fusion
  574.1 29.3 %all-gather.38.cloned.1.call-done = bf16[1,1024,1024]{2,1,0:T(8,128)(2,1)} async-done(((bf16[1,256,1024]{2,1,0:T(8,128)(2,1)}), bf16[1,1024,1024]{2,1,0:T(8,128)(2,1)}) %all-gather.38.cloned.1.call-update) | async-done | bytes 2097168 | tf_op jit(solution)/shard_map/all_gather | solution.py:278
  608.6 10.1 fusion.102
  648.2 46.0 %reduce-scatter.28.cloned.1.call-done = bf16[256,1024]{1,0:T(8,128)(2,1)} async-done(((bf16[1024,1024]{1,0:T(8,128)(2,1)}), bf16[256,1024]{1,0:T(8,128)(2,1)}) %reduce-scatter.28.cloned.1.call-update) | async-done | bytes 524304 | tf_op jit(solution)/shard_map/reduce_scatter | solution.py:287
  697.0 42.6 %reduce-scatter.26.cloned.1.call-done = bf16[256,1024]{1,0:T(8,128)(2,1)} async-done(((bf16[1024,1024]{1,0:T(8,128)(2,1)}), bf16[256,1024]{1,0:T(8,128)(2,1)}) %reduce-scatter.26.cloned.1.call-update) | async-done | bytes 524304 | tf_op jit(solution)/shard_map/reduce_scatter | solution.py:260
  744.9 43.8 %all-gather.36.cloned.1.call-done = bf16[1024,1024]{1,0:T(8,128)(2,1)} async-done(((bf16[256,1024]{1,0:T(8,128)(2,1)}), bf16[1024,1024]{1,0:T(8,128)(2,1)}) %all-gather.36.cloned.1.call-update) | async-done | bytes 2097168 | tf_op jit(solution)/shard_map/all_gather | solution.py:297
  793.7 34.4 %while.31 = (s32[]{:T(128)}, f32[1024,2,2,64]{0,3,2,1:T(8,128)S(1)}, bf16[4096,2,64]{0,2,1:T(8,128)(2,1)}, bf16[4096,2,64]{0,2,1:T(8,128)(2,1)}, s32[]{:T(128)},...) while((s32[]{:T(128)}, ...), condition=%wide.region_33.35_spmd.clone, body=%wide.region_32.34_spmd.clone.sunk | while | flops 2728003584 | bytes 93126936 | solution.py:155
  793.7 9.3 fusion.345
  803.7 9.3 fusion.346
  841.2 33.8 %while.30 = (s32[]{:T(128)}, f32[1024,2,2,64]{0,3,2,1:T(8,128)S(1)}, bf16[4096,2,64]{0,2,1:T(8,128)(2,1)}, bf16[4096,2,64]{0,2,1:T(8,128)(2,1)}, s32[]{:T(128)},...) while((s32[]{:T(128)}, ...), condition=%wide.region_23.25_spmd.clone, body=%wide.region_22.24_spmd.clone.sunk | while | flops 2728003584 | bytes 99418456 | solution.py:155
  841.4 9.2 fusion.330
  851.3 9.5 fusion.331
  888.2 66.5 %reduce-scatter.38.cloned.1.call-done = bf16[1024,2,64]{0,2,1:T(8,128)(2,1)} async-done(((bf16[4096,2,64]{0,2,1:T(8,128)(2,1)}), bf16[1024,2,64]{0,2,1:T(8,128)(2,1)}) %reduce-scatter.38.cloned.1.call-update) | async-done | bytes 262160 | tf_op jit(solution)/shard_map/reduce_scatter | solution.py:312
  955.8 139.6 %reduce-scatter.30.cloned.1.call-done = bf16[1024,2,64]{0,2,1:T(8,128)(2,1)} async-done(((bf16[4096,2,64]{0,2,1:T(8,128)(2,1)}), bf16[1024,2,64]{0,2,1:T(8,128)(2,1)}) %reduce-scatter.30.cloned.1.call-update) | async-done | bytes 262160 | tf_op jit(solution)/shard_map/reduce_scatter | solution.py:312
  1102.6 20.4 %reduce-scatter.40.cloned.1.call-done = bf16[1024,2,64]{0,2,1:T(8,128)(2,1)} async-done(((bf16[4096,2,64]{0,2,1:T(8,128)(2,1)}), bf16[1024,2,64]{0,2,1:T(8,128)(2,1)}) %reduce-scatter.40.cloned.1.call-update) | async-done | bytes 262160 | tf_op jit(solution)/shard_map/reduce_scatter | solution.py:315
  1134.3 16.1 reduce-scatter.32.cloned.1.call-done
  1210.8 31.9 %reduce-scatter.34.cloned.1.call-done = bf16[256,1024]{1,0:T(8,128)(2,1)} async-done(((bf16[1024,1024]{1,0:T(8,128)(2,1)}), bf16[256,1024]{1,0:T(8,128)(2,1)}) %reduce-scatter.34.cloned.1.call-update) | async-done | bytes 524304 | tf_op jit(solution)/shard_map/reduce_scatter | solution.py:331
  1244.9 43.4 %reduce-scatter.22.cloned.1.call-done = bf16[256,1024]{1,0:T(8,128)(2,1)} async-done(((bf16[1024,1024]{1,0:T(8,128)(2,1)}), bf16[256,1024]{1,0:T(8,128)(2,1)}) %reduce-scatter.22.cloned.1.call-update) | async-done | bytes 524304 | tf_op jit(solution)/shard_map/reduce_scatter | solution.py:260
  1291.6 39.9 %all-reduce.8 = (f32[1024]{0:T(1024)}, f32[1024]{0:T(1024)}, f32[64]{0:T(128)}, f32[64]{0:T(128)}) all-reduce(f32[1024]{0:T(1024)S(1)} %add.382, f32[1024]{0:T(1024)S(1)} %add.383, f32[64]{0:T(128)S(1)} %add.384, f32[64]{0:T(128)S(1)} %add.385), channel_id=1, replica_groups=mesh['shard'=2,'ctx'=4,'tp'=4] {'shard','ctx','tp'}, use_global_device_ids=true, to_apply=%region_49.51 | all-reduce | flops 2176 | bytes 17408 | tf_op jit(solution)/shard_map/psum | solution.py:352
  1337.2 8.9 reduce-scatter.54.cloned.1.call-done
  1346.1 58.2 %reduce-scatter.52.cloned.1.call-done = f32[128,1152]{1,0:T(8,128)} async-done(((f32[1024,1152]{1,0:T(8,128)}), f32[128,1152]{1,0:T(8,128)}) %reduce-scatter.52.cloned.1.call-update) | async-done | bytes 589840 | tf_op jit(solution)/shard_map/reduce_scatter | solution.py:348
  1404.3 57.9 %reduce-scatter.56.cloned.1.call-done = f32[1152,128]{1,0:T(8,128)} async-done(((f32[1152,1024]{1,0:T(8,128)}), f32[1152,128]{1,0:T(8,128)}) %reduce-scatter.56.cloned.1.call-update) | async-done | bytes 589840 | tf_op jit(solution)/shard_map/reduce_scatter | solution.py:350
  1462.2 40.1 %reduce-scatter.50.cloned.1.call-done = f32[256,128]{1,0:T(8,128)} async-done(((f32[256,1024]{1,0:T(8,128)}), f32[256,128]{1,0:T(8,128)}) %reduce-scatter.50.cloned.1.call-update) | async-done | bytes 131088 | tf_op jit(solution)/shard_map/reduce_scatter | solution.py:347
  1502.3 40.0 %reduce-scatter.44.cloned.1.call-done = f32[128,256]{1,0:T(8,128)} async-done(((f32[1024,256]{1,0:T(8,128)}), f32[128,256]{1,0:T(8,128)}) %reduce-scatter.44.cloned.1.call-update) | async-done | bytes 131088 | tf_op jit(solution)/shard_map/reduce_scatter | solution.py:344
  1542.3 38.1 %reduce-scatter.48.cloned.1.call-done = f32[128,128]{1,0:T(8,128)} async-done(((f32[1024,128]{1,0:T(8,128)}), f32[128,128]{1,0:T(8,128)}) %reduce-scatter.48.cloned.1.call-update) | async-done | bytes 65552 | tf_op jit(solution)/shard_map/reduce_scatter | solution.py:346
  1580.4 37.8 %reduce-scatter.46.cloned.1.call-done = f32[128,128]{1,0:T(8,128)} async-done(((f32[1024,128]{1,0:T(8,128)}), f32[128,128]{1,0:T(8,128)}) %reduce-scatter.46.cloned.1.call-update) | async-done | bytes 65552 | tf_op jit(solution)/shard_map/reduce_scatter | solution.py:345
  (475 shorter events, 302.8 us)
Async XLA Ops:
  7.2 54.0 %all-gather.16.cloned.1.call-start = ((), (), s32[]{:S(2)}) async-start(), calls=%async_computation.19 | async-start | bytes 2621440 | tf_op jit(solution)/shard_map/all_gather | solution.py:204
  12.4 95.5 %all-gather.28.cloned.1.call-start = ((), (), s32[]{:S(2)}) async-start(), calls=%async_computation.27 | async-start | bytes 2621440 | tf_op jit(solution)/shard_map/all_gather | solution.py:204
  13.2 151.4 %all-gather.30.cloned.1.call-start = ((), (), s32[]{:S(2)}) async-start(), calls=%async_computation.28 | async-start | bytes 1310720 | tf_op jit(solution)/shard_map/all_gather | solution.py:82
  112.4 52.2 %all-gather.32.cloned.1.call-start = ((), (), s32[]{:S(2)}) async-start(), calls=%async_computation.29 | async-start | bytes 1310720 | tf_op jit(solution)/shard_map/all_gather | solution.py:83
  125.3 127.8 %all-gather.18.cloned.1.call-start = ((), (), s32[]{:S(2)}) async-start(), calls=%async_computation.20 | async-start | bytes 1310720 | tf_op jit(solution)/shard_map/all_gather | solution.py:82
  137.4 115.8 %all-gather.20.cloned.1.call-start = ((), (), s32[]{:S(2)}) async-start(), calls=%async_computation.21 | async-start | bytes 1310720 | tf_op jit(solution)/shard_map/all_gather | solution.py:83
  155.7 188.1 %reduce-scatter.24.cloned.1.call-start = ((), (), s32[]{:S(2)}) async-start(), calls=%async_computation.30 | async-start | bytes 2621440 | tf_op jit(solution)/shard_map/reduce_scatter | solution.py:231
  252.9 129.7 %reduce-scatter.20.cloned.1.call-start = ((), (), s32[]{:S(2)}) async-start(), calls=%async_computation.22 | async-start | bytes 2621440 | tf_op jit(solution)/shard_map/reduce_scatter | solution.py:231
  339.6 124.6 %all-gather.40.cloned.1.call-start = ((), (), s32[]{:S(2)}) async-start(), calls=%async_computation.50 | async-start | bytes 2621440 | tf_op jit(solution)/shard_map/all_gather | solution.py:278
  341.9 151.7 %all-gather.26.cloned.1.call-start = ((), (), s32[]{:S(2)}) async-start(), calls=%async_computation.25 | async-start | bytes 2654208 | tf_op jit(solution)/shard_map/all_gather | solution.py:68
  342.5 182.0 %all-gather.24.cloned.1.call-start = ((), (), s32[]{:S(2)}) async-start(), calls=%async_computation.24 | async-start | bytes 2654208 | tf_op jit(solution)/shard_map/all_gather | solution.py:67
  343.2 212.1 %all-gather.22.cloned.1.call-start = ((), (), s32[]{:S(2)}) async-start(), calls=%async_computation.23 | async-start | bytes 2654208 | tf_op jit(solution)/shard_map/all_gather | solution.py:66
  343.8 259.6 %all-gather.38.cloned.1.call-start = ((), (), s32[]{:S(2)}) async-start(), calls=%async_computation.49 | async-start | bytes 2621440 | tf_op jit(solution)/shard_map/all_gather | solution.py:278
  384.2 355.4 %copy-start.98 = (f32[256]{0:T(256)}, f32[256]{0:T(256)S(1)}, u32[]{:S(2)}) copy-start(f32[256]{0:T(256)S(1)} %fusion.170) | copy-start | bytes 3076
  384.2 355.4 %copy-start.96 = (f32[256]{0:T(256)}, f32[256]{0:T(256)S(1)}, u32[]{:S(2)}) copy-start(f32[256]{0:T(256)S(1)} %fusion.172) | copy-start | bytes 3076
  385.8 22.9 %collective-permute-start.3 = (bf16[256,1024]{1,0:T(8,128)(2,1)S(1)}, bf16[256,1024]{1,0:T(8,128)(2,1)}, u32[]{:S(2)}, u32[]{:S(2)}) collective-permute-start(bf16[256,1024]{1,0:T(8,128)(2,1)S(1)} %get-tuple-element.346), channel_id=1, source_target_pairs={{0,1},{1,2},{2,3},{3,0},{4,5},{5,6},{6,7},{7,4},{8,9},{9,10},{10,1... | collective-permute-start | bytes 1572872 | tf_op jit(solution)/shard_map/ppermute | solution.py:249
  385.9 45.2 %collective-permute-start = (bf16[256,1024]{1,0:T(8,128)(2,1)S(1)}, bf16[256,1024]{1,0:T(8,128)(2,1)S(1)}, u32[]{:S(2)}, u32[]{:S(2)}) collective-permute-start(bf16[256,1024]{1,0:T(8,128)(2,1)S(1)} %get-tuple-element.345), channel_id=1, source_target_pairs={{0,1},{1,2},{2,3},{3,0},{4,5},{5,6},{6,7},{7,4},{8,9},{9,10},{10,1... | collective-permute-start | bytes 1572872 | tf_op jit(solution)/shard_map/ppermute | solution.py:249
  408.8 44.9 %collective-permute-start.4 = (bf16[256,1024]{1,0:T(8,128)(2,1)}, bf16[256,1024]{1,0:T(8,128)(2,1)}, u32[]{:S(2)}, u32[]{:S(2)}) collective-permute-start(bf16[256,1024]{1,0:T(8,128)(2,1)} %collective-permute-done.3), channel_id=1, source_target_pairs={{0,1},{1,2},{2,3},{3,0},{4,5},{5,6},{6,7},{7,4},{8,9},{9,10},{10,1... | collective-permute-start | bytes 1572872 | tf_op jit(solution)/shard_map/ppermute | solution.py:249
  411.0 237.2 %reduce-scatter.36.cloned.1.call-start = ((), (), s32[]{:S(2)}) async-start(), calls=%async_computation.37 | async-start | bytes 2621440 | tf_op jit(solution)/shard_map/reduce_scatter | solution.py:287
  431.1 69.8 %collective-permute-start.1 = (bf16[256,1024]{1,0:T(8,128)(2,1)S(1)}, bf16[256,1024]{1,0:T(8,128)(2,1)}, u32[]{:S(2)}, u32[]{:S(2)}) collective-permute-start(bf16[256,1024]{1,0:T(8,128)(2,1)S(1)} %collective-permute-done), channel_id=1, source_target_pairs={{0,1},{1,2},{2,3},{3,0},{4,5},{5,6},{6,7},{7,4},{8,9},{9,10},{10,1... | collective-permute-start | bytes 1572872 | tf_op jit(solution)/shard_map/ppermute | solution.py:249
  453.7 49.1 %collective-permute-start.5 = (bf16[256,1024]{1,0:T(8,128)(2,1)}, bf16[256,1024]{1,0:T(8,128)(2,1)}, u32[]{:S(2)}, u32[]{:S(2)}) collective-permute-start(bf16[256,1024]{1,0:T(8,128)(2,1)} %collective-permute-done.4), channel_id=1, source_target_pairs={{0,1},{1,2},{2,3},{3,0},{4,5},{5,6},{6,7},{7,4},{8,9},{9,10},{10,1... | collective-permute-start | bytes 1572872 | tf_op jit(solution)/shard_map/ppermute | solution.py:249
  501.0 107.7 %collective-permute-start.2 = (bf16[256,1024]{1,0:T(8,128)(2,1)}, bf16[256,1024]{1,0:T(8,128)(2,1)}, u32[]{:S(2)}, u32[]{:S(2)}) collective-permute-start(bf16[256,1024]{1,0:T(8,128)(2,1)} %collective-permute-done.1), channel_id=1, source_target_pairs={{0,1},{1,2},{2,3},{3,0},{4,5},{5,6},{6,7},{7,4},{8,9},{9,10},{10,1... | collective-permute-start | bytes 1572872 | tf_op jit(solution)/shard_map/ppermute | solution.py:249
  574.1 120.1 %reduce-scatter.28.cloned.1.call-start = ((), (), s32[]{:S(2)}) async-start(), calls=%async_computation.32 | async-start | bytes 2621440 | tf_op jit(solution)/shard_map/reduce_scatter | solution.py:287
  634.6 105.0 %reduce-scatter.26.cloned.1.call-start = ((), (), s32[]{:S(2)}) async-start(), calls=%async_computation.31 | async-start | bytes 2621440 | tf_op jit(solution)/shard_map/reduce_scatter | solution.py:260
  641.7 146.9 %all-gather.36.cloned.1.call-start = ((), (), s32[]{:S(2)}) async-start(), calls=%async_computation.38 | async-start | bytes 2621440 | tf_op jit(solution)/shard_map/all_gather | solution.py:297
  743.2 92.2 %all-gather.34.cloned.1.call-start = ((), (), s32[]{:S(2)}) async-start(), calls=%async_computation.33 | async-start | bytes 2621440 | tf_op jit(solution)/shard_map/all_gather | solution.py:297
  744.8 209.9 %reduce-scatter.38.cloned.1.call-start = ((), (), s32[]{:S(2)}) async-start(), calls=%async_computation.39 | async-start | bytes 1310720 | tf_op jit(solution)/shard_map/reduce_scatter | solution.py:312
  828.1 267.3 %reduce-scatter.30.cloned.1.call-start = ((), (), s32[]{:S(2)}) async-start(), calls=%async_computation.34 | async-start | bytes 1310720 | tf_op jit(solution)/shard_map/reduce_scatter | solution.py:312
  875.0 248.0 %reduce-scatter.40.cloned.1.call-start = ((), (), s32[]{:S(2)}) async-start(), calls=%async_computation.40 | async-start | bytes 1310720 | tf_op jit(solution)/shard_map/reduce_scatter | solution.py:315
  878.5 272.0 %reduce-scatter.32.cloned.1.call-start = ((), (), s32[]{:S(2)}) async-start(), calls=%async_computation.35 | async-start | bytes 1310720 | tf_op jit(solution)/shard_map/reduce_scatter | solution.py:315
  885.3 210.2 %copy-start.43 = (f32[1024,64]{0,1:T(8,128)S(1)}, f32[1024,64]{0,1:T(8,128)}, u32[]{:S(2)}) copy-start(f32[1024,64]{0,1:T(8,128)} %copy-done.42) | copy-start | bytes 786436
  885.3 211.3 %copy-start.18 = (f32[1024,128]{0,1:T(8,128)S(1)}, f32[1024,128]{0,1:T(8,128)}, u32[]{:S(2)}) copy-start(f32[1024,128]{0,1:T(8,128)} %copy-done.17) | copy-start | bytes 1572868
  885.3 211.3 %copy-start.20 = (f32[1024,128]{0,1:T(8,128)S(1)}, f32[1024,128]{0,1:T(8,128)}, u32[]{:S(2)}) copy-start(f32[1024,128]{0,1:T(8,128)} %copy-done.19) | copy-start | bytes 1572868
  885.3 211.3 %copy-start.31 = (f32[1024,64]{0,1:T(8,128)S(1)}, f32[1024,64]{0,1:T(8,128)}, u32[]{:S(2)}) copy-start(f32[1024,64]{0,1:T(8,128)} %copy-done.28) | copy-start | bytes 786436
  885.3 211.3 %copy-start.81 = (f32[1024,2]{0,1:T(2,128)S(1)}, f32[1024,2]{0,1:T(2,128)}, u32[]{:S(2)}) copy-start(f32[1024,2]{0,1:T(2,128)} %copy-done.80) | copy-start | bytes 24580
  885.3 211.3 %copy-start.83 = (f32[1024,2]{0,1:T(2,128)S(1)}, f32[1024,2]{0,1:T(2,128)}, u32[]{:S(2)}) copy-start(f32[1024,2]{0,1:T(2,128)} %copy-done.82) | copy-start | bytes 24580
  885.3 211.3 %copy-start.118 = (f32[64]{0:T(128)S(1)}, f32[64]{0:T(128)}, u32[]{:S(2)}) copy-start(f32[64]{0:T(128)} %param.31) | copy-start | bytes 772
  888.1 210.1 %copy-start.87 = (f32[1024,2]{0,1:T(2,128)S(1)}, f32[1024,2]{0,1:T(2,128)}, u32[]{:S(2)}) copy-start(f32[1024,2]{0,1:T(2,128)} %copy-done.86) | copy-start | bytes 24580
  888.1 322.6 %reduce-scatter.42.cloned.1.call-start = ((), (), s32[]{:S(2)}) async-start(), calls=%async_computation.41 | async-start | bytes 2621440 | tf_op jit(solution)/shard_map/reduce_scatter | solution.py:331
  1128.7 114.0 %reduce-scatter.34.cloned.1.call-start = ((), (), s32[]{:S(2)}) async-start(), calls=%async_computation.36 | async-start | bytes 2621440 | tf_op jit(solution)/shard_map/reduce_scatter | solution.py:331
  1156.1 132.2 %reduce-scatter.22.cloned.1.call-start = ((), (), s32[]{:S(2)}) async-start(), calls=%async_computation.26 | async-start | bytes 2621440 | tf_op jit(solution)/shard_map/reduce_scatter | solution.py:260
  1162.8 183.3 %reduce-scatter.54.cloned.1.call-start = ((), (), s32[]{:S(2)}) async-start(), calls=%async_computation.47 | async-start | bytes 5308416 | tf_op jit(solution)/shard_map/reduce_scatter | solution.py:349
  1173.5 230.7 %reduce-scatter.52.cloned.1.call-start = ((), (), s32[]{:S(2)}) async-start(), calls=%async_computation.46 | async-start | bytes 5308416 | tf_op jit(solution)/shard_map/reduce_scatter | solution.py:348
  1183.9 278.3 %reduce-scatter.56.cloned.1.call-start = ((), (), s32[]{:S(2)}) async-start(), calls=%async_computation.48 | async-start | bytes 5308416 | tf_op jit(solution)/shard_map/reduce_scatter | solution.py:350
  1193.5 308.8 %reduce-scatter.50.cloned.1.call-start = ((), (), s32[]{:S(2)}) async-start(), calls=%async_computation.45 | async-start | bytes 1179648 | tf_op jit(solution)/shard_map/reduce_scatter | solution.py:347
  1200.2 342.1 %reduce-scatter.44.cloned.1.call-start = ((), (), s32[]{:S(2)}) async-start(), calls=%async_computation.42 | async-start | bytes 1179648 | tf_op jit(solution)/shard_map/reduce_scatter | solution.py:344
  1203.8 376.7 %reduce-scatter.48.cloned.1.call-start = ((), (), s32[]{:S(2)}) async-start(), calls=%async_computation.44 | async-start | bytes 589824 | tf_op jit(solution)/shard_map/reduce_scatter | solution.py:346
  1207.4 410.8 %reduce-scatter.46.cloned.1.call-start = ((), (), s32[]{:S(2)}) async-start(), calls=%async_computation.43 | async-start | bytes 589824 | tf_op jit(solution)/shard_map/reduce_scatter | solution.py:345
  (122 other events, 3405.2 us)
Sparse Core Ops, SparseCore 0:
  12.5 48.6 all-gather.15
  63.3 44.5 all-gather.27
  112.5 15.5 all-gather.29
  129.5 17.2 all-gather.31
  148.8 18.1 all-gather.17
  169.0 16.7 all-gather.19
  253.0 42.7 reduce-scatter.23
  339.7 42.8 reduce-scatter.19
  384.7 79.4 all-gather.39
  465.9 27.6 all-gather.25
  495.5 29.0 all-gather.23
  526.3 29.0 all-gather.21
  557.5 45.9 all-gather.37
  605.6 42.5 reduce-scatter.35
  651.0 43.1 reduce-scatter.27
  696.4 43.1 reduce-scatter.25
  743.4 45.2 all-gather.35
  790.7 44.6 all-gather.33
  838.1 116.5 reduce-scatter.37
  957.6 137.7 reduce-scatter.29
  1098.1 24.8 reduce-scatter.39
  1125.5 24.8 reduce-scatter.31
  1152.9 43.8 reduce-scatter.41
  1199.5 43.1 reduce-scatter.33
  1245.1 43.1 reduce-scatter.21
  1292.2 53.8 reduce-scatter.53
  1350.3 53.8 reduce-scatter.51
  1408.3 53.8 reduce-scatter.55
  1466.3 35.9 reduce-scatter.49
  1506.3 36.0 reduce-scatter.43
  1546.3 34.1 reduce-scatter.47
  1584.1 34.1 reduce-scatter.45
